TPU v7x, 32 devices: a whole 2x2x4 slice. The times are simulated.
32 devices in a mesh: groups: 1, frames: 32 (over z, y, x, core).
Axes of the slice: x: 2, y: 2, z: 4, core: 2. Of those that a mesh axis runs over, the one named last changes fastest.
Arguments:
- skip: bfloat16 [32, 256, 640], P(('groups', 'frames')), may hold values from -24 to 24
- control: bfloat16 [32, 256, 640], P('groups', 'frames'), may hold values from -6 to 6
- zero_weight: bfloat16 [640, 640], replicated, may hold values from -1 to 1
- gn_gain: float32 [640], replicated, may hold values from 0.1 to 1.9
- gn_bias: float32 [640], replicated, may hold values from -0.5 to 0.5
- conv_weight: bfloat16 [9, 640, 640], replicated, may hold values from -0.078125 to 0.078125
- ln_gain: float32 [640], replicated, may hold values from 0.1 to 1.9
- qkv_weight: bfloat16 [640, 1920], replicated, may hold values from -5 to 5
- out_weight: bfloat16 [640, 640], replicated, may hold values from -0.25 to 0.25
Outputs:
- output: bfloat16 [32, 256, 640], P(('groups', 'frames'))
All inputs are finite; a program needn't handle non-finite values.
Results may differ from a plain program's by a relative error of at most 0.0043.
Values may be sent and summed in bfloat16 or wider, within the bound.
No kernel may reach another device: no remote copies, remote signals or barrier semaphores. Data moves between devices by JAX's collectives and lax.ppermute only.
A program may use at most 64 MiB of HBM per device.

v0:
```python
import math
import jax
import jax.numpy as jnp
from jax import lax
from jax.sharding import PartitionSpec as P

HEADS = 10
HD = 64
GROUPS = 32
CLIP = 32
W = 32
norm_epsilon = 1e-05


def attend_block(qkv_rows, chans):
    frame_count, single, count, _ = qkv_rows.shape
    clip_count = frame_count // CLIP
    shaped = qkv_rows.reshape(clip_count, CLIP, count, 3, HEADS, HD)
    queries = shaped[:, :, :, 0]
    key_rows = shaped[:, :, :, 1]
    value_rows = shaped[:, :, :, 2]
    scores = jnp.einsum(
        "atphd,asphd->aphts", queries, key_rows, preferred_element_type=jnp.float32
    ) * (1.0 / math.sqrt(HD))
    scores = scores - jnp.max(scores, axis=-1, keepdims=True)
    expon = jnp.exp(scores)
    attn_weights = (expon / jnp.sum(expon, axis=-1, keepdims=True)).astype(jnp.bfloat16)
    mixed = jnp.einsum(
        "aphts,asphd->atphd", attn_weights, value_rows, preferred_element_type=jnp.float32
    )
    return mixed.astype(jnp.bfloat16).reshape(frame_count, single, count, chans)


def body(
    skip, control, zero_weight, gn_gain, gn_bias, conv_weight, ln_gain, qkv_weight, out_weight
):
    f_dev, pixels, chans = skip.shape
    devices = lax.axis_size("frames")
    frame_count, pix_dev, _ = control.shape
    height = pixels // W
    zero_out = jnp.dot(control.reshape(-1, chans), zero_weight, preferred_element_type=jnp.float32)
    zero_out = zero_out.astype(jnp.bfloat16).reshape(frame_count, pix_dev, chans)
    zero_frames = lax.all_to_all(zero_out, "frames", split_axis=0, concat_axis=1, tiled=True)
    joined = skip.astype(jnp.float32) + zero_frames.astype(jnp.float32)
    group_size = chans // GROUPS
    grouped = joined.reshape(f_dev, pixels, GROUPS, group_size)
    clip_count = f_dev * devices // CLIP
    frame_ids = lax.axis_index("frames") * f_dev + jnp.arange(f_dev, dtype=jnp.int32)
    member = (
        frame_ids[:, None] // CLIP == jnp.arange(clip_count, dtype=jnp.int32)[None, :]
    ).astype(jnp.float32)
    count_all = float(CLIP * pixels * group_size)
    frame_sums = jnp.sum(grouped, axis=(1, 3))
    clip_sums = jnp.sum(member[:, :, None] * frame_sums[:, None, :], axis=0)
    frame_sq = jnp.sum(jnp.square(grouped), axis=(1, 3))
    clip_sq = jnp.sum(member[:, :, None] * frame_sq[:, None, :], axis=0)
    total_sums, total_sq = lax.psum((clip_sums, clip_sq), "frames")
    clip_mean = total_sums / count_all
    clip_var = total_sq / count_all - jnp.square(clip_mean)
    frame_mean = jnp.sum(member[:, :, None] * clip_mean[None], axis=1)
    centred = grouped - frame_mean[:, None, :, None]
    frame_var = jnp.sum(member[:, :, None] * clip_var[None], axis=1)
    normed_groups = (centred * lax.rsqrt(frame_var + norm_epsilon)[:, None, :, None]).reshape(
        f_dev, pixels, chans
    )
    activated = (
        jax.nn.silu(normed_groups * gn_gain + gn_bias)
        .astype(jnp.bfloat16)
        .reshape(f_dev, height, W, chans)
    )
    padded = jnp.pad(activated, ((0, 0), (1, 1), (1, 1), (0, 0)))
    conv_sum = jnp.zeros((f_dev * pixels, chans), jnp.float32)
    for tap_index in range(9):
        row_shift, col_shift = divmod(tap_index, 3)
        window = padded[:, row_shift : row_shift + height, col_shift : col_shift + W, :].reshape(
            -1, chans
        )
        conv_sum = conv_sum + jnp.dot(
            window, conv_weight[tap_index], preferred_element_type=jnp.float32
        )
    resid = joined.reshape(-1, chans) + conv_sum
    token_mean = jnp.mean(resid, axis=-1, keepdims=True)
    token_var = jnp.mean(jnp.square(resid - token_mean), axis=-1, keepdims=True)
    normed = ((resid - token_mean) * lax.rsqrt(token_var + norm_epsilon) * ln_gain).astype(
        jnp.bfloat16
    )
    per_device = pixels // devices
    qkv_rows = jnp.dot(normed, qkv_weight, preferred_element_type=jnp.float32).astype(jnp.bfloat16)
    qkv_rows = qkv_rows.reshape(f_dev, devices, per_device, 3 * chans)
    attended = attend_block(
        lax.all_to_all(qkv_rows, "frames", split_axis=1, concat_axis=0, tiled=True), chans
    )
    returned = lax.all_to_all(attended, "frames", split_axis=0, concat_axis=1, tiled=True)
    output = resid + jnp.dot(
        returned.reshape(-1, chans), out_weight, preferred_element_type=jnp.float32
    )
    return output.astype(jnp.bfloat16).reshape(f_dev, pixels, chans)


def solution(mesh):
    in_specs = (
        P(("groups", "frames"), None, None),
        P("groups", "frames", None),
        P(),
        P(),
        P(),
        P(),
        P(),
        P(),
        P(),
    )
    out_specs = P(("groups", "frames"), None, None)
    return jax.shard_map(body, mesh=mesh, in_specs=in_specs, out_specs=out_specs, check_vma=False)
```

profile of v0, /device:TPU:0, one launch (start us, length us, event | category | flops | bytes accessed | tf_op | source)
XLA Modules:
  0.0 136.1 jit_solution(5476533162441262583)
XLA Ops:
  0.0 0.0 copy-start
  0.0 0.0 copy-start.2
  0.0 2.6 %fusion.7 = bf16[32,8,640]{2,1,0:T(8,128)(2,1)} fusion(bf16[640,640]{1,0:T(8,128)(2,1)} %param.11, bf16[32,8,640]{2,1,0:T(8,128)(2,1)} %param.10), kind=kOutput, calls=%fused_computation.21 | convolution fusion | flops 209879040 | bytes 1474560 | tf_op jit(solution)/shard_map/dot_general | solution.py:41
  2.6 7.3 %all-to-all-start = ((bf16[32,8,640]{2,1,0:T(8,128)(2,1)}), bf16[32,8,640]{2,1,0:T(8,128)(2,1)S(1)}, u32[]{:S(2)}, u32[]{:S(2)}) async-start(bf16[32,8,640]{2,1,0:T(8,128)(2,1)} %fusion.7), calls=%async_computation | async-start | bytes 655360 | tf_op jit(solution)/shard_map/all_to_all | solution.py:43
  9.9 12.0 %all-to-all-done = bf16[32,8,640]{2,1,0:T(8,128)(2,1)S(1)} async-done(((bf16[32,8,640]{2,1,0:T(8,128)(2,1)}), bf16[32,8,640]{2,1,0:T(8,128)(2,1)S(1)}, u32[]{:S(2)}, u32[]{:S(2)}) %all-to-all-start) | async-done | bytes 327712 | tf_op jit(solution)/shard_map/all_to_all | solution.py:43
  22.0 1.1 multiply_reduce_fusion.1
  23.1 0.1 reduce_sum.79
  23.2 0.1 reduce_sum.76
  23.3 0.1 reduce_sum.80
  23.4 0.1 reduce_sum.77
  23.5 38.5 %all-reduce.1 = (f32[1,32]{1,0:T(1,128)S(1)}, f32[1,32]{1,0:T(1,128)S(1)}) all-reduce(f32[1,32]{1,0:T(1,128)S(1)} %get-tuple-element.27, f32[1,32]{1,0:T(1,128)S(1)} %get-tuple-element.26), channel_id=1, replica_groups=mesh['groups'=1,'frames'=32] {'frames'}, use_global_device_ids=true, to_apply=%region_2.3 | all-reduce | flops 64 | bytes 512 | tf_op jit(solution)/shard_map/psum | solution.py:57
  62.0 0.1 sub.45
  62.1 0.1 sub.46
  62.2 0.1 mul.144
  62.3 0.1 mul.145
  62.4 0.0 copy-done.2
  62.4 0.0 copy-start.1
  62.4 1.1 multiply_convert_fusion.1
  63.5 0.3 pad_slice_fusion
  63.8 2.0 %fusion.17 = f32[256,640]{1,0:T(8,128)S(1)} fusion(bf16[256,640]{1,0:T(8,128)(2,1)S(1)} %bitcast.123, bf16[9,640,640]{2,1,0:T(8,128)(2,1)} %param.14), kind=kOutput, calls=%fused_computation.31 | convolution fusion | flops 209715200 | bytes 1802240 | tf_op jit(solution)/shard_map/dot_general | solution.py:78
  65.8 1.6 %convolution_add_fusion.8 = f32[256,640]{1,0:T(8,128)S(1)} fusion(f32[256,640]{1,0:T(8,128)S(1)} %fusion.17, bf16[256,640]{1,0:T(8,128)(2,1)S(1)} %bitcast.122, bf16[9,640,640]{2,1,0:T(8,128)(2,1)} %param.14), kind=kOutput, calls=%fused_computation.17 | convolution fusion | flops 209879040 | bytes 2457600 | tf_op jit(solution)/shard_map/dot_general | solution.py:78
  67.4 0.0 copy-done.1
  67.4 0.5 convolution_add_fusion.7
  67.9 0.5 convolution_add_fusion.6
  68.3 0.5 convolution_add_fusion.5
  68.8 0.0 copy-start.3
  68.8 0.5 convolution_add_fusion.4
  69.3 0.5 convolution_add_fusion.3
  69.7 0.0 copy-start.4
  69.8 0.5 convolution_add_fusion.2
  70.2 0.0 copy-done.3
  70.2 0.6 fusion.39
  70.8 0.2 multiply_reduce_fusion
  71.0 0.0 copy-done
  71.0 0.0 copy-done.4
  71.1 1.0 fusion.1
  72.1 28.4 %all_to_all.12 = bf16[1,32,8,1920]{3,2,0,1:T(8,128)(2,1)} all-to-all(bf16[1,32,8,1920]{3,2,0,1:T(8,128)(2,1)S(1)} %fusion.1), channel_id=1, replica_groups=mesh['groups'=1,'frames'=32] {'frames'}, dimensions={1} | all-to-all | bytes 1966080 | tf_op jit(solution)/shard_map/all_to_all | solution.py:91
  100.5 4.4 %reshape.253 = bf16[1,32,8,3,10,64]{5,4,3,2,1,0:T(8,128)(2,1)} reshape(bf16[1,32,8,1920]{3,2,0,1:T(8,128)(2,1)} %all_to_all.12) | data formatting | bytes 1966080 | tf_op jit(solution)/shard_map/reshape | solution.py:18
  104.9 4.2 %fusion.38 = (bf16[1,32,8,1,10,64]{5,4,3,2,1,0:T(8,128)(2,1)}, bf16[1,32,8,1,10,64]{5,4,3,2,1,0:T(8,128)(2,1)}, bf16[1,32,8,1,10,64]{5,4,3,2,1,0:T(8,128)(2,1)}) fusion(bf16[1,32,8,3,10,64]{5,4,3,2,1,0:T(8,128)(2,1)} %reshape.253), kind=kLoop, calls=%fused_computation.74 | loop fusion | bytes 1966080 | tf_op jit(solution)/shard_map/slice | solution.py:21
  109.1 3.8 %fusion.40 = (f32[8,10,32]{2,1,0:T(8,128)S(1)}, f32[8,10,32,32]{2,3,1,0:T(8,128)}) fusion(bf16[1,32,8,1,10,64]{5,4,3,2,1,0:T(8,128)(2,1)} %get-tuple-element.11, bf16[1,32,8,1,10,64]{5,4,3,2,1,0:T(8,128)(2,1)} %get-tuple-element.10), kind=kOutput, calls=%fused_computation.76 | convolution fusion | flops 10731551 | bytes 993280 | tf_op jit(solution)/shard_map/sub | solution.py:25
  112.9 2.3 %fusion.4 = bf16[1,32,8,10,64]{4,1,3,2,0:T(8,128)(2,1)S(1)} fusion(f32[8,10,32,32]{2,3,1,0:T(8,128)} %get-tuple-element.25, bf16[1,32,8,1,10,64]{5,4,3,2,1,0:T(8,128)(2,1)} %get-tuple-element.9, f32[8,10,32]{2,1,0:T(8,128)S(1)} %get-tuple-element.24), kind=kOutput, calls=%fused_computation.8 | convolution fusion | flops 10813440 | bytes 993280 | tf_op jit(solution)/shard_map/aphts,asphd->atphd/dot_general | solution.py:28
  115.1 1.3 copy.21
  116.5 1.8 %reshape.257 = bf16[32,1,8,640]{3,2,0,1:T(8,128)(2,1)S(1)} reshape(bf16[1,32,8,10,64]{4,3,2,1,0:T(8,128)(2,1)} %copy.21) | data formatting | bytes 655360 | tf_op jit(solution)/shard_map/reshape | solution.py:31
  118.3 15.5 %all_to_all.13 = bf16[32,1,8,640]{3,2,1,0:T(8,128)(2,1)S(1)} all-to-all(bf16[32,1,8,640]{3,2,1,0:T(8,128)(2,1)S(1)} %bitcast.116), channel_id=1, replica_groups=mesh['groups'=1,'frames'=32] {'frames'}, dimensions={0} | all-to-all | bytes 655360 | tf_op jit(solution)/shard_map/all_to_all | solution.py:93
  133.8 2.3 %fusion.8 = bf16[1,256,640]{2,1,0:T(8,128)(2,1)} fusion(f32[256,640]{1,0:T(8,128)S(1)} %get-tuple-element.23, bf16[640,640]{1,0:T(8,128)(2,1)} %param.17, bf16[32,1,8,640]{3,2,1,0:T(8,128)(2,1)S(1)} %all_to_all.13), kind=kOutput, calls=%fused_computation.22 | convolution fusion | flops 210042880 | bytes 2129920 | tf_op jit(solution)/shard_map/dot_general | solution.py:94
  (4 shorter events, 0.0 us)
Async XLA Ops:
  0.0 71.0 %copy-start = (bf16[640,1920]{1,0:T(8,128)(2,1)S(1)}, bf16[640,1920]{1,0:T(8,128)(2,1)}, u32[]{:S(2)}) copy-start(bf16[640,1920]{1,0:T(8,128)(2,1)} %param.16) | copy-start | bytes 7372804
  0.0 62.4 %copy-start.2 = (bf16[1,256,640]{2,1,0:T(8,128)(2,1)S(1)}, bf16[1,256,640]{2,1,0:T(8,128)(2,1)}, u32[]{:S(2)}) copy-start(bf16[1,256,640]{2,1,0:T(8,128)(2,1)} %param.9) | copy-start | bytes 983044
  2.6 19.4 %all-to-all-start = ((bf16[32,8,640]{2,1,0:T(8,128)(2,1)}), bf16[32,8,640]{2,1,0:T(8,128)(2,1)S(1)}, u32[]{:S(2)}, u32[]{:S(2)}) async-start(bf16[32,8,640]{2,1,0:T(8,128)(2,1)} %fusion.7), calls=%async_computation | async-start | bytes 655360 | tf_op jit(solution)/shard_map/all_to_all | solution.py:43
  62.4 5.0 %copy-start.1 = (bf16[9,640,640]{2,1,0:T(8,128)(2,1)S(1)}, bf16[9,640,640]{2,1,0:T(8,128)(2,1)}, u32[]{:S(2)}) copy-start(bf16[9,640,640]{2,1,0:T(8,128)(2,1)} %param.14) | copy-start | bytes 22118404
  68.8 1.4 %copy-start.3 = (bf16[1,256,640]{2,1,0:T(8,128)(2,1)S(1)}, bf16[1,256,640]{2,1,0:T(8,128)(2,1)}, u32[]{:S(2)}) copy-start(bf16[1,256,640]{2,1,0:T(8,128)(2,1)} %param.9) | copy-start | bytes 983044
  69.7 1.3 copy-start.4
where the time goes:
time: 137 us; the launch traced here: 136 us
  blocking collectives  82.4 us (60%)
  matrix products  18.8 us (14%)
  local copies, waits for them, and re-layouts  12.6 us (9%)
  waiting for transfers between devices  12 us (9%)
  starting transfers between devices  7.33 us (5%)
  other arithmetic  2.73 us (2%)
    psum x1, blocking collectives, body(): total_sums, total_sq = lax.psum((clip_sums, clip_sq), 'frames')  38.5 us
    all_to_all x1, blocking collectives, body(): lax.all_to_all(qkv_rows, 'frames', split_axis=1, concat_axis=0, tiled=True)  28.4 us
    all_to_all x1, blocking collectives, body(): lax.all_to_all(attended, 'frames', split_axis=0, concat_axis=1, tiled=True)  15.5 us
    all_to_all x1, waiting for transfers between devices, body(): lax.all_to_all(zero_out, 'frames', split_axis=0, concat_axis=1, tiled=True)  12 us
    all_to_all x1, starting transfers between devices, body(): lax.all_to_all(zero_out, 'frames', split_axis=0, concat_axis=1, tiled=True)  7.33 us
    dot_general x9, matrix products, body(): jnp.dot(window, conv_weight[tap_index], preferred_element_type=jnp.float32)  6.89 us
    reshape x1, local copies, waits for them, and re-layouts, attend_block(): shaped = qkv_rows.reshape(clip_count, CLIP, count, 3, HEADS, HD)  4.38 us
    slice x1, local copies, waits for them, and re-layouts, attend_block(): value_rows = shaped[:, :, :, 2]  4.21 us
  transfers between devices with their start and end apart: 1, of which 1 were waited for; matrix products, arithmetic and copies ran while one was open for 0% of the time, Pallas kernels for 0%

commit v1 on v0

--- a/solution.py
+++ b/solution.py
@@ -90,7 +90,12 @@
     attended = attend_block(
         lax.all_to_all(qkv_rows, "frames", split_axis=1, concat_axis=0, tiled=True), chans
     )
-    returned = lax.all_to_all(attended, "frames", split_axis=0, concat_axis=1, tiled=True)
+    returned = jnp.concatenate(
+        lax.all_to_all(
+            jnp.stack(jnp.split(attended, lax.axis_size("frames"), axis=0)), "frames", 0, 0
+        ),
+        axis=1,
+    )
     output = resid + jnp.dot(
         returned.reshape(-1, chans), out_weight, preferred_element_type=jnp.float32
     )

time: 137 us -> 183 us (1.34)
  local copies, waits for them, and re-layouts: 12.6 us -> 57 us
    another operation x0 -> x33, local copies, waits for them, and re-layouts: none -> 28.7 us  [body(): jnp.stack(jnp.split(attended, lax.axis_size('frames'), axis=0))]
    unnamed x10 -> x41, local copies, waits for them, and re-layouts: 0.03 us -> 13.6 us
    split x0 -> x2, local copies, waits for them, and re-layouts: none -> 5.28 us  [body(): jnp.split(attended, lax.axis_size('frames'), axis=0)]
    reshape x1 -> x0, local copies, waits for them, and re-layouts: 1.83 us -> none  [attend_block(): return mixed.astype(jnp.bfloat16).reshape(frame_count, single, count, chans)]
where the time goes in v1:
time: 183 us; the launch traced here: 181 us
  blocking collectives  82.4 us (45%)
  local copies, waits for them, and re-layouts  57 us (31%)
  matrix products  18.9 us (10%)
  waiting for transfers between devices  12 us (7%)
  starting transfers between devices  7.32 us (4%)
  other arithmetic  2.73 us (1%)
    psum x1, blocking collectives, body(): total_sums, total_sq = lax.psum((clip_sums, clip_sq), 'frames')  38.5 us
    another operation x33, local copies, waits for them, and re-layouts, body(): jnp.stack(jnp.split(attended, lax.axis_size('frames'), axis=0))  28.7 us
    all_to_all x1, blocking collectives, body(): lax.all_to_all(qkv_rows, 'frames', split_axis=1, concat_axis=0, tiled=True)  28.4 us
    all_to_all x1, blocking collectives, body(): lax.all_to_all(jnp.stack(jnp.split(attended, lax.axis_size('frames'), axi...  15.5 us
    unnamed x41, local copies, waits for them, and re-layouts  13.6 us
    all_to_all x1, waiting for transfers between devices, body(): lax.all_to_all(zero_out, 'frames', split_axis=0, concat_axis=1, tiled=True)  12 us
    all_to_all x1, starting transfers between devices, body(): lax.all_to_all(zero_out, 'frames', split_axis=0, concat_axis=1, tiled=True)  7.32 us
    dot_general x9, matrix products, body(): jnp.dot(window, conv_weight[tap_index], preferred_element_type=jnp.float32)  6.9 us
  transfers between devices with their start and end apart: 1, of which 1 were waited for; matrix products, arithmetic and copies ran while one was open for 0% of the time, Pallas kernels for 0%

profile of v1, /device:TPU:0, one launch (start us, length us, event | category | flops | bytes accessed | tf_op | source)
XLA Modules:
  0.0 180.5 jit_solution(1538507992161779389)
XLA Ops:
  0.0 2.6 %fusion.7 = bf16[32,8,640]{2,1,0:T(8,128)(2,1)} fusion(bf16[640,640]{1,0:T(8,128)(2,1)} %param.11, bf16[32,8,640]{2,1,0:T(8,128)(2,1)} %param.10), kind=kOutput, calls=%fused_computation.21 | convolution fusion | flops 209879040 | bytes 1474560 | tf_op jit(solution)/shard_map/dot_general | solution.py:41
  2.6 7.3 %all-to-all-start = ((bf16[32,8,640]{2,1,0:T(8,128)(2,1)}), bf16[32,8,640]{2,1,0:T(8,128)(2,1)S(1)}, u32[]{:S(2)}, u32[]{:S(2)}) async-start(bf16[32,8,640]{2,1,0:T(8,128)(2,1)} %fusion.7), calls=%async_computation | async-start | bytes 655360 | tf_op jit(solution)/shard_map/all_to_all | solution.py:43
  9.9 12.0 %all-to-all-done = bf16[32,8,640]{2,1,0:T(8,128)(2,1)S(1)} async-done(((bf16[32,8,640]{2,1,0:T(8,128)(2,1)}), bf16[32,8,640]{2,1,0:T(8,128)(2,1)S(1)}, u32[]{:S(2)}, u32[]{:S(2)}) %all-to-all-start) | async-done | bytes 327712 | tf_op jit(solution)/shard_map/all_to_all | solution.py:43
  22.0 1.1 multiply_reduce_fusion.1
  23.5 38.5 %all-reduce.1 = (f32[1,32]{1,0:T(1,128)S(1)}, f32[1,32]{1,0:T(1,128)S(1)}) all-reduce(f32[1,32]{1,0:T(1,128)S(1)} %get-tuple-element.59, f32[1,32]{1,0:T(1,128)S(1)} %get-tuple-element.58), channel_id=1, replica_groups=mesh['groups'=1,'frames'=32] {'frames'}, use_global_device_ids=true, to_apply=%region_2.3 | all-reduce | flops 64 | bytes 512 | tf_op jit(solution)/shard_map/psum | solution.py:57
  62.4 1.1 multiply_convert_fusion.1
  63.8 2.0 %fusion.17 = f32[256,640]{1,0:T(8,128)S(1)} fusion(bf16[256,640]{1,0:T(8,128)(2,1)S(1)} %bitcast.121, bf16[9,640,640]{2,1,0:T(8,128)(2,1)} %param.14), kind=kOutput, calls=%fused_computation.31 | convolution fusion | flops 209715200 | bytes 1802240 | tf_op jit(solution)/shard_map/dot_general | solution.py:78
  65.8 1.6 convolution_add_fusion.8
  71.1 1.0 fusion.1
  72.1 28.4 %all_to_all.23 = bf16[1,32,8,1920]{3,2,0,1:T(8,128)(2,1)} all-to-all(bf16[1,32,8,1920]{3,2,0,1:T(8,128)(2,1)S(1)} %fusion.1), channel_id=1, replica_groups=mesh['groups'=1,'frames'=32] {'frames'}, dimensions={1} | all-to-all | bytes 1966080 | tf_op jit(solution)/shard_map/all_to_all | solution.py:91
  100.5 4.4 %reshape.308 = bf16[1,32,8,3,10,64]{5,4,3,2,1,0:T(8,128)(2,1)} reshape(bf16[1,32,8,1920]{3,2,0,1:T(8,128)(2,1)} %all_to_all.23) | data formatting | bytes 1966080 | tf_op jit(solution)/shard_map/reshape | solution.py:18
  104.9 4.2 %fusion.38 = (bf16[1,32,8,1,10,64]{5,4,3,2,1,0:T(8,128)(2,1)}, bf16[1,32,8,1,10,64]{5,4,3,2,1,0:T(8,128)(2,1)}, bf16[1,32,8,1,10,64]{5,4,3,2,1,0:T(8,128)(2,1)}) fusion(bf16[1,32,8,3,10,64]{5,4,3,2,1,0:T(8,128)(2,1)} %reshape.308), kind=kLoop, calls=%fused_computation.138 | loop fusion | bytes 1966080 | tf_op jit(solution)/shard_map/slice | solution.py:21
  109.1 3.8 %fusion.40 = (f32[8,10,32]{2,1,0:T(8,128)S(1)}, f32[8,10,32,32]{2,3,1,0:T(8,128)}) fusion(bf16[1,32,8,1,10,64]{5,4,3,2,1,0:T(8,128)(2,1)} %get-tuple-element.43, bf16[1,32,8,1,10,64]{5,4,3,2,1,0:T(8,128)(2,1)} %get-tuple-element.42), kind=kOutput, calls=%fused_computation.140 | convolution fusion | flops 10731551 | bytes 993280 | tf_op jit(solution)/shard_map/sub | solution.py:25
  112.9 2.3 %fusion.4 = bf16[1,32,8,10,64]{4,1,3,2,0:T(8,128)(2,1)S(1)} fusion(f32[8,10,32,32]{2,3,1,0:T(8,128)} %get-tuple-element.57, bf16[1,32,8,1,10,64]{5,4,3,2,1,0:T(8,128)(2,1)} %get-tuple-element.41, f32[8,10,32]{2,1,0:T(8,128)S(1)} %get-tuple-element.56), kind=kOutput, calls=%fused_computation.8 | convolution fusion | flops 10813440 | bytes 993280 | tf_op jit(solution)/shard_map/aphts,asphd->atphd/dot_general | solution.py:28
  115.1 2.3 %slice_reduce_fusion.19 = (bf16[8,10,64]{2,1,0:T(8,128)(2,1)}, bf16[8,10,64]{2,1,0:T(8,128)(2,1)}, bf16[8,10,64]{2,1,0:T(8,128)(2,1)}, bf16[8,10,64]{2,1,0:T(8,1...) fusion(bf16[1,32,8,10,64]{4,1,3,2,0:T(8,128)(2,1)S(1)} %fusion.4), kind=kLoop, calls=%fused_computation.117 | loop fusion | bytes 266240 | tf_op jit(solution)/shard_map/split | solution.py:95
  117.4 3.0 %slice_reduce_fusion = (bf16[8,10,64]{2,1,0:T(8,128)(2,1)}, bf16[8,10,64]{2,1,0:T(8,128)(2,1)}, bf16[8,10,64]{2,1,0:T(8,128)(2,1)}, bf16[8,10,64]{2,1,0:T(8,128)...) fusion(bf16[1,32,8,10,64]{4,1,3,2,0:T(8,128)(2,1)S(1)} %fusion.4), kind=kLoop, calls=%fused_computation.98 | loop fusion | bytes 389120 | tf_op jit(solution)/shard_map/split | solution.py:95
  120.4 0.9 stack.130
  121.2 1.4 stack.111
  122.7 1.4 stack.110
  124.1 1.4 stack.109
  125.6 1.4 stack.108
  127.0 1.4 stack.107
  128.5 1.4 stack.106
  129.9 1.4 stack.105
  131.4 1.4 stack.104
  132.8 1.4 stack.103
  134.2 1.5 stack.102
  135.7 1.4 stack.101
  137.1 1.4 stack.100
  138.6 1.4 stack.99
  140.0 1.4 stack.129
  141.5 1.4 stack.128
  142.9 1.4 stack.127
  144.4 1.4 stack.126
  145.8 1.4 stack.125
  149.1 0.7 constant_dynamic-update-slice_fusion.31
  149.8 0.7 constant_dynamic-update-slice_fusion.30
  150.5 0.7 constant_dynamic-update-slice_fusion.29
  152.0 0.7 constant_dynamic-update-slice_fusion.27
  154.1 0.7 constant_dynamic-update-slice_fusion.24
  156.2 0.7 constant_dynamic-update-slice_fusion.21
  156.9 0.7 constant_dynamic-update-slice_fusion.20
  158.5 0.7 constant_dynamic-update-slice_fusion.6
  159.2 0.7 constant_dynamic-update-slice_fusion.5
  161.3 0.7 constant_dynamic-update-slice_fusion.2
  162.0 0.7 constant_dynamic-update-slice_fusion.1
  162.7 15.5 %all_to_all.24 = bf16[32,1,1,8,640]{4,3,2,1,0:T(8,128)(2,1)S(1)} all-to-all(bf16[32,1,1,8,640]{4,3,2,1,0:T(8,128)(2,1)S(1)} %constant_dynamic-update-slice_fusion), channel_id=1, replica_groups=mesh['groups'=1,'frames'=32] {'frames'}, dimensions={0} | all-to-all | bytes 655360 | tf_op jit(solution)/shard_map/all_to_all | solution.py:94
  178.2 2.3 %fusion.8 = bf16[1,256,640]{2,1,0:T(8,128)(2,1)} fusion(f32[256,640]{1,0:T(8,128)S(1)} %get-tuple-element.55, bf16[640,640]{1,0:T(8,128)(2,1)} %param.17, bf16[32,1,1,8,640]{4,3,2,1,0:T(8,128)(2,1)S(1)} %all_to_all.24), kind=kOutput, calls=%fused_computation.22 | convolution fusion | flops 210042880 | bytes 2129920 | tf_op jit(solution)/shard_map/dot_general | solution.py:99
  (65 shorter events, 12.3 us)
Async XLA Ops:
  0.0 71.0 %copy-start = (bf16[640,1920]{1,0:T(8,128)(2,1)S(1)}, bf16[640,1920]{1,0:T(8,128)(2,1)}, u32[]{:S(2)}) copy-start(bf16[640,1920]{1,0:T(8,128)(2,1)} %param.16) | copy-start | bytes 7372804
  0.0 62.4 %copy-start.2 = (bf16[1,256,640]{2,1,0:T(8,128)(2,1)S(1)}, bf16[1,256,640]{2,1,0:T(8,128)(2,1)}, u32[]{:S(2)}) copy-start(bf16[1,256,640]{2,1,0:T(8,128)(2,1)} %param.9) | copy-start | bytes 983044
  2.6 19.4 %all-to-all-start = ((bf16[32,8,640]{2,1,0:T(8,128)(2,1)}), bf16[32,8,640]{2,1,0:T(8,128)(2,1)S(1)}, u32[]{:S(2)}, u32[]{:S(2)}) async-start(bf16[32,8,640]{2,1,0:T(8,128)(2,1)} %fusion.7), calls=%async_computation | async-start | bytes 655360 | tf_op jit(solution)/shard_map/all_to_all | solution.py:43
  62.4 5.0 %copy-start.1 = (bf16[9,640,640]{2,1,0:T(8,128)(2,1)S(1)}, bf16[9,640,640]{2,1,0:T(8,128)(2,1)}, u32[]{:S(2)}) copy-start(bf16[9,640,640]{2,1,0:T(8,128)(2,1)} %param.14) | copy-start | bytes 22118404
  68.8 1.4 copy-start.3
  69.7 1.3 copy-start.4
